TPU v7x, 256 devices: a whole 4x4x8 slice. The times are simulated.
256 devices in a mesh: dp: 8 (over y_hi, x), ctx: 32 (over y_lo, z, core).
Axes of the slice: x: 4, y: 4 (y_hi: 2, y_lo: 2; y = y_hi * 2 + y_lo), z: 8, core: 2. Of those that a mesh axis runs over, the one named last changes fastest.
Arguments:
- mixed: bfloat16 [8192, 4096], P('ctx', 'dp'), may hold values from -6 to 6
- log_decay: float32 [8192, 16], P('ctx', 'dp'), may hold values from -1 to 0
- beta_logit: float32 [8192, 16], P('ctx', 'dp'), may hold values from -4 to 4
- conv_weight: float32 [4, 4096], P(None, 'dp'), may hold values from -3 to 3
- norm_gain: float32 [128], replicated, may hold values from 0.1 to 1.9
- out_weight: bfloat16 [2048, 1024], P('dp'), may hold values from -0.125 to 0.125
- out_grad: bfloat16 [8192, 1024], P(('ctx', 'dp')), may hold values from -12 to 12
Outputs:
- output: bfloat16 [8192, 1024], P(('ctx', 'dp'))
- grad_mixed: bfloat16 [8192, 4096], P('ctx', 'dp')
- grad_log_decay: float32 [8192, 16], P('ctx', 'dp')
- grad_beta_logit: float32 [8192, 16], P('ctx', 'dp')
- grad_conv_weight: float32 [4, 4096], P(None, 'dp')
- grad_norm_gain: float32 [128], replicated
- grad_out_weight: float32 [2048, 1024], P(('dp', 'ctx'))
All inputs are finite; a program needn't handle non-finite values.
Results may differ from a plain program's by a relative error of at most 0.03.
Values may be sent and summed in bfloat16 or wider, within the bound.
No kernel may reach another device: no remote copies, remote signals or barrier semaphores. Data moves between devices by JAX's collectives and lax.ppermute only.
A program may use at most 128 MiB of HBM per device.

v0:
```python
import math
import jax
import jax.numpy as jnp
from jax import lax
from jax.sharding import PartitionSpec as P

VHEADS = 16
KHEADS = 8
HEADDIM = 128
BLOCK = 64
EPS = 1e-06
HIGHEST = lax.Precision.HIGHEST


def shifted(block, axis, distance):
    devices = range(lax.axis_size(axis))
    route = [(i - distance, i) for i in devices if i - distance in devices]
    return lax.ppermute(block, axis, route)


def prefix_2(value, axis, join, neutral, backward):
    count, mine = (lax.axis_size(axis), lax.axis_index(axis))
    pieces = jax.tree.map(lambda part: lax.all_gather(part, axis), value)
    if backward:
        pieces = jax.tree.map(lambda part: part[::-1], pieces)
        mine = count - 1 - mine
    total = jax.tree.map(
        lambda part, zero: jnp.full_like(part, 0) + jnp.asarray(zero, part.dtype), value, neutral
    )

    def step(position, total):
        longer = join(total, jax.tree.map(lambda part: part[position], pieces))
        return jax.tree.map(lambda new, old: jnp.where(position < mine, new, old), longer, total)

    return lax.fori_loop(0, count - 1, step, total)


def product(pattern, left_array, right_array):
    return jnp.einsum(pattern, left_array, right_array, precision=HIGHEST)


def conv_silu(padded_rows, conv_weight):
    conv_taps = conv_weight.shape[0]
    row_count = padded_rows.shape[0] - (conv_taps - 1)
    summed = jnp.zeros((row_count, padded_rows.shape[1]), jnp.float32)
    for offset in range(conv_taps):
        summed = summed + conv_weight[offset] * padded_rows[offset : offset + row_count]
    return jax.nn.silu(summed)


def unit_rows(vectors):
    return vectors * lax.rsqrt(jnp.sum(vectors * vectors, axis=-1, keepdims=True) + EPS)


def prepare(active, decays, strengths):
    row_count = active.shape[0]
    value_heads = decays.shape[1]
    group_size = VHEADS // KHEADS
    key_heads = value_heads // group_size
    grouped = active.reshape(row_count, key_heads, (2 + group_size) * HEADDIM)
    queries = unit_rows(grouped[:, :, :HEADDIM]) * (1.0 / math.sqrt(HEADDIM))
    key_rows = unit_rows(grouped[:, :, HEADDIM : 2 * HEADDIM])
    values = grouped[:, :, 2 * HEADDIM :].reshape(row_count, value_heads, HEADDIM)
    queries = jnp.repeat(queries, group_size, axis=1)
    key_rows = jnp.repeat(key_rows, group_size, axis=1)
    blocks = row_count // BLOCK

    def arrange(tensor):
        return jnp.transpose(tensor.reshape(blocks, BLOCK, value_heads, -1), (0, 2, 1, 3))

    return (
        arrange(queries),
        arrange(key_rows),
        arrange(values),
        arrange(decays[:, :, None])[..., 0],
        arrange(jax.nn.sigmoid(strengths)[:, :, None])[..., 0],
    )


def block_terms(block_in):
    queries, key_rows, values, decays, strengths = (
        block_in[0],
        block_in[1],
        block_in[2],
        block_in[3],
        block_in[4],
    )
    length = decays.shape[-1]
    cumulative = jnp.cumsum(decays, axis=-1)
    row_index = lax.broadcasted_iota(jnp.int32, (length, length), 0)
    col_index = lax.broadcasted_iota(jnp.int32, (length, length), 1)
    causal = row_index >= col_index
    strict = row_index > col_index
    spread = cumulative[:, :, None] - cumulative[:, None, :]
    damping = jnp.where(causal, jnp.exp(jnp.where(causal, spread, 0.0)), 0.0)
    key_inner = product("hck,hsk->hcs", key_rows, key_rows)
    lower_mat = jnp.where(strict, strengths[:, :, None] * damping * key_inner, 0.0)
    growth = jnp.exp(cumulative)
    tail_keys = jnp.exp(cumulative[:, -1:] - cumulative)[..., None] * key_rows
    stacked = jnp.concatenate(
        [(strengths * growth)[..., None] * key_rows, strengths[..., None] * values], axis=-1
    )
    solved = lax.linalg.triangular_solve(
        lower_mat, stacked, left_side=True, lower=True, unit_diagonal=True
    )
    head_size = key_rows.shape[-1]
    write_keys = solved[..., :head_size]
    new_values = solved[..., head_size:]
    scores = damping * product("hck,hsk->hcs", queries, key_rows)
    return (write_keys, new_values, scores, growth, tail_keys, queries, growth[:, -1])


def rows_layout(stacked):
    return jnp.transpose(stacked, (0, 2, 1, 3)).reshape(
        stacked.shape[0] * stacked.shape[2], stacked.shape[1], stacked.shape[3]
    )


def run_blocks(carry_state, arranged):

    def run_advance(running, block_in):
        write_keys, new_values, scores, growth, tail_keys, queries, growth_end = block_terms(
            block_in
        )
        deltas = new_values - product("hck,hek->hce", write_keys, running)
        output = growth[..., None] * product("hck,hek->hce", queries, running) + product(
            "hcs,hse->hce", scores, deltas
        )
        next_state = growth_end[:, None, None] * running + product(
            "hse,hsk->hek", deltas, tail_keys
        )
        return (next_state, output)

    final_state, outputs = lax.scan(run_advance, carry_state, arranged)
    return (rows_layout(outputs), final_state)


def local_core(carry_state, active, decays, strengths):
    return run_blocks(carry_state, prepare(active, decays, strengths))


def eye_stack(value_heads):
    return jnp.broadcast_to(jnp.eye(HEADDIM, dtype=jnp.float32), (value_heads, HEADDIM, HEADDIM))


def local_pieces(active, decays, strengths):
    identity = eye_stack(decays.shape[1])
    start_carry = (identity, jnp.zeros((decays.shape[1], HEADDIM, HEADDIM), jnp.float32))

    def local_advance(running, block_in):
        through, offset_state = running
        write_keys, new_values, scores, growth, tail_keys, queries, growth_end = block_terms(
            block_in
        )
        effective = growth[..., None] * queries - product("hcs,hsk->hck", scores, write_keys)
        local_out = product("hck,hek->hce", effective, offset_state) + product(
            "hcs,hse->hce", scores, new_values
        )
        reach_rows = product("hck,hjk->hcj", effective, through)
        block_map = growth_end[:, None, None] * identity - product(
            "hsk,hsj->hkj", write_keys, tail_keys
        )
        block_add = product("hse,hsk->hek", new_values, tail_keys)
        through = product("hjk,hkl->hjl", through, block_map)
        offset_state = product("hek,hkl->hel", offset_state, block_map) + block_add
        return ((through, offset_state), (local_out, reach_rows))

    final_pair, outputs = lax.scan(local_advance, start_carry, prepare(active, decays, strengths))
    return (rows_layout(outputs[0]), rows_layout(outputs[1]), final_pair[0], final_pair[1])


def normalize(mixer_out, gain_vector):
    scaled = (
        mixer_out
        * lax.rsqrt(jnp.mean(mixer_out * mixer_out, axis=-1, keepdims=True) + EPS)
        * gain_vector
    )
    return scaled.reshape(mixer_out.shape[0], -1)


def chain_step(earlier_pair, later_pair):
    return (
        product("hjk,hkl->hjl", earlier_pair[0], later_pair[0]),
        product("hek,hkl->hel", earlier_pair[1], later_pair[0]) + later_pair[1],
    )


def local(mixed, log_decay, beta_logit, conv_weight, norm_gain, out_weight, out_grad):
    conv_taps = conv_weight.shape[0]
    row_count = mixed.shape[0]
    value_heads = log_decay.shape[1]
    rim_rows = shifted(mixed[row_count - (conv_taps - 1) :], "ctx", 1)
    padded = jnp.concatenate([rim_rows, mixed], axis=0).astype(jnp.float32)
    active_wide, conv_pull = jax.vjp(conv_silu, padded, conv_weight)
    active = lax.optimization_barrier(active_wide.astype(jnp.bfloat16)).astype(jnp.float32)
    start_pair = (eye_stack(value_heads), jnp.zeros((value_heads, HEADDIM, HEADDIM), jnp.float32))
    pieces_out = local_pieces(active, log_decay, beta_logit)
    chain_maps, chain_adds = (pieces_out[2], pieces_out[3])
    prefix = prefix_2((chain_maps, chain_adds), "ctx", chain_step, start_pair, False)
    entry_state = prefix[1]
    core_out, core_pull = jax.vjp(local_core, entry_state, active, log_decay, beta_logit)
    mixer_out, leaving = core_out
    normed_wide, norm_pull = jax.vjp(normalize, mixer_out, norm_gain)
    normed = normed_wide.astype(jnp.bfloat16)
    result = lax.psum_scatter(
        jnp.dot(normed, out_weight, preferred_element_type=jnp.float32).astype(jnp.bfloat16),
        "dp",
        scatter_dimension=0,
        tiled=True,
    )
    full_grad = lax.all_gather(out_grad, "dp", axis=0, tiled=True)
    back_rows = jnp.dot(full_grad, out_weight.T, preferred_element_type=jnp.float32)
    grad_weight = lax.psum_scatter(
        jnp.einsum("tv,td->vd", normed, full_grad, preferred_element_type=jnp.float32).astype(
            jnp.bfloat16
        ),
        "ctx",
        scatter_dimension=0,
        tiled=True,
    ).astype(jnp.float32)
    grad_mixer, grad_gain = norm_pull(back_rows)
    local_grad = core_pull((grad_mixer, jnp.zeros_like(leaving)))[0]
    suffix = prefix_2(
        (jnp.swapaxes(chain_maps, 1, 2), local_grad), "ctx", chain_step, start_pair, True
    )
    exit_grad = suffix[1]
    core_grads = core_pull((grad_mixer, exit_grad))
    grad_active, grad_decay, grad_beta = (core_grads[1], core_grads[2], core_grads[3])
    grad_padded, grad_conv = conv_pull(grad_active)
    spill_rows = shifted(grad_padded[: conv_taps - 1], "ctx", -1)
    own_rows = grad_padded[conv_taps - 1 :]
    own_rows = own_rows.at[row_count - (conv_taps - 1) :].add(spill_rows)
    grad_conv_total, gain_partial = lax.psum((grad_conv, grad_gain), "ctx")
    grad_gain_total = lax.psum(gain_partial, "dp")
    return (
        result,
        own_rows.astype(jnp.bfloat16),
        grad_decay,
        grad_beta,
        grad_conv_total,
        grad_gain_total,
        grad_weight,
    )


def solution(mesh):
    return jax.shard_map(
        local,
        mesh=mesh,
        in_specs=(
            P("ctx", "dp"),
            P("ctx", "dp"),
            P("ctx", "dp"),
            P(None, "dp"),
            P(),
            P("dp", None),
            P(("ctx", "dp"), None),
        ),
        out_specs=(
            P(("ctx", "dp"), None),
            P("ctx", "dp"),
            P("ctx", "dp"),
            P("ctx", "dp"),
            P(None, "dp"),
            P(),
            P(("dp", "ctx"), None),
        ),
        check_vma=False,
    )
```

profile of v0, /device:TPU:8, one launch (start us, length us, event | category | flops | bytes accessed | tf_op | source)
XLA Modules:
  0.0 858.3 jit_solution(8584469403035977819)
XLA Ops:
  8.0 1.9 collective-permute-start
  12.5 3.9 collective-permute-done
  20.2 52.3 %while.145 = (s32[]{:T(128)}, f32[2,128,128]{1,2,0:T(8,128)S(1)}, f32[2,128,128]{1,2,0:T(8,128)S(1)}, f32[4,2,64]{2,1,0:T(2,128)S(1)}, f32[4,2,64]{2,1,0:T(2,128...) while((s32[]{:T(128)}, f32[2,128,128]{1,2,0:T(8,128)S(1)}, ...), condition=%wide.region_3.5_spmd.clone, body=%wide.region_1.4_spmd.clone.sunk | while | flops 189067456 | bytes 2523331 | solution.py:168
  21.2 9.8 %custom-call.44 = f32[2,1,64,64]{2,3,1,0:T(8,128)S(1)} custom-call(f32[2,1,64,64]{3,2,1,0:T(8,128)S(1)} %fusion.384), custom_call_target="InvertDiagBlocksLowerTriangular" | custom-call | tf_op jit(solution)/shard_map/while/body/eval_jaxpr/triangular_solve/custom-call.1 | solution.py:103
  34.3 9.8 %custom-call.44 = f32[2,1,64,64]{2,3,1,0:T(8,128)S(1)} custom-call(f32[2,1,64,64]{3,2,1,0:T(8,128)S(1)} %fusion.384), custom_call_target="InvertDiagBlocksLowerTriangular" | custom-call | tf_op jit(solution)/shard_map/while/body/eval_jaxpr/triangular_solve/custom-call.1 | solution.py:103
  47.3 9.8 %custom-call.44 = f32[2,1,64,64]{2,3,1,0:T(8,128)S(1)} custom-call(f32[2,1,64,64]{3,2,1,0:T(8,128)S(1)} %fusion.384), custom_call_target="InvertDiagBlocksLowerTriangular" | custom-call | tf_op jit(solution)/shard_map/while/body/eval_jaxpr/triangular_solve/custom-call.1 | solution.py:103
  60.4 9.8 %custom-call.44 = f32[2,1,64,64]{2,3,1,0:T(8,128)S(1)} custom-call(f32[2,1,64,64]{3,2,1,0:T(8,128)S(1)} %fusion.384), custom_call_target="InvertDiagBlocksLowerTriangular" | custom-call | tf_op jit(solution)/shard_map/while/body/eval_jaxpr/triangular_solve/custom-call.1 | solution.py:103
  74.3 35.2 %all_gather.33 = bf16[256,1024]{1,0:T(8,128)(2,1)S(1)} all-gather(bf16[32,1024]{1,0:T(8,128)(2,1)S(1)} %copy-done.9), channel_id=1, replica_groups=mesh['dp'=8,'ctx'=32] {'dp'}, dimensions={0}, use_global_device_ids=true | all-gather | bytes 589824 | tf_op jit(solution)/shard_map/all_gather | solution.py:211
  111.7 28.6 %all-gather.9.cloned.1.call-done = f32[64,128,128]{2,1,0:T(8,128)} async-done(((f32[2,128,128]{2,1,0:T(8,128)}), f32[64,128,128]{2,1,0:T(8,128)}) %all-gather.9.cloned.1.call-update) | async-done | bytes 4194320 | tf_op jit(solution)/shard_map/all_gather | solution.py:23
  140.3 68.5 %all-gather.11.cloned.1.call-done = f32[64,128,128]{2,1,0:T(8,128)} async-done(((f32[2,128,128]{2,1,0:T(8,128)}), f32[64,128,128]{2,1,0:T(8,128)}) %all-gather.11.cloned.1.call-update) | async-done | bytes 4194320 | tf_op jit(solution)/shard_map/all_gather | solution.py:23
  208.8 73.6 %while.146 = (s32[]{:T(128)}, f32[2,128,128]{1,2,0:T(8,128)S(1)}, s32[]{:T(128)}, f32[32,2,128,128]{3,2,1,0:T(8,128)}, f32[32,2,128,128]{3,2,1,0:T(8,128)}, /*index=5*/s32[]{:T(128)}, s32[]{:T(128)}) while((s32[]{:T(128)}, f32[2,128,128]{1,2,0:T(8,128)S(1)}, s32[]{:T(128)}, f32[32,2,128,128]{3,2,1,0:T(8,128)}, ...), condition=%wide.region_5.7_spmd.clone, body=%wide.region_4.6_spmd.clone.sunk | while | flops 50462724 | bytes 1443947 | solution.py:35
  287.1 97.9 %while.143 = (s32[]{:T(128)}, f32[2,128,128]{2,1,0:T(8,128)S(1)}, f32[4,2,64,128]{3,2,1,0:T(8,128)}, f32[4,2,64,64]{3,2,1,0:T(8,128)}, f32[4,2,64,64]{3,2,1,0:T(...) while((s32[]{:T(128)}, f32[2,128,128]{2,1,0:T(8,128)S(1)}, ...), condition=%wide.region_9.11_spmd.clone.clone, body=%wide.region_7.10_spmd.clone.clone.sunk | while | flops 138834496 | bytes 3687305 | solution.py:134
  292.7 11.2 %custom-call.42 = f32[2,1,64,64]{2,3,1,0:T(8,128)} custom-call(f32[2,1,64,64]{3,2,1,0:T(8,128)} %get-tuple-element.3230), custom_call_target="InvertDiagBlocksLowerTriangular" | custom-call | tf_op jit(solution)/shard_map/jvp()/while/body/eval_jaxpr/triangular_solve/custom-call.1 | solution.py:103
  303.9 1.8 bitcast_dynamic-update-slice_fusion.19
  317.2 11.2 %custom-call.42 = f32[2,1,64,64]{2,3,1,0:T(8,128)} custom-call(f32[2,1,64,64]{3,2,1,0:T(8,128)} %get-tuple-element.3230), custom_call_target="InvertDiagBlocksLowerTriangular" | custom-call | tf_op jit(solution)/shard_map/jvp()/while/body/eval_jaxpr/triangular_solve/custom-call.1 | solution.py:103
  328.4 1.8 bitcast_dynamic-update-slice_fusion.19
  341.6 11.2 %custom-call.42 = f32[2,1,64,64]{2,3,1,0:T(8,128)} custom-call(f32[2,1,64,64]{3,2,1,0:T(8,128)} %get-tuple-element.3230), custom_call_target="InvertDiagBlocksLowerTriangular" | custom-call | tf_op jit(solution)/shard_map/jvp()/while/body/eval_jaxpr/triangular_solve/custom-call.1 | solution.py:103
  352.8 1.8 bitcast_dynamic-update-slice_fusion.19
  366.1 11.2 %custom-call.42 = f32[2,1,64,64]{2,3,1,0:T(8,128)} custom-call(f32[2,1,64,64]{3,2,1,0:T(8,128)} %get-tuple-element.3230), custom_call_target="InvertDiagBlocksLowerTriangular" | custom-call | tf_op jit(solution)/shard_map/jvp()/while/body/eval_jaxpr/triangular_solve/custom-call.1 | solution.py:103
  377.3 1.8 bitcast_dynamic-update-slice_fusion.19
  390.1 2.2 convolution_convert_fusion
  392.4 18.6 %while.147 = (s32[]{:T(128)}, f32[2,128,128]{2,1,0:T(8,128)S(1)}, f32[4,2,1,1]{1,3,2,0:T(1,128)}, f32[4,2,64,1]{2,1,3,0:T(2,128)S(1)}, f32[4,2,64,128]{3,2,1,0:T...) while((s32[]{:T(128)}, f32[2,128,128]{2,1,0:T(8,128)S(1)}, ...), condition=%wide.region_14.16_spmd.clone, body=%wide.region_13.15_spmd.clone.sunk | while | flops 88293376 | bytes 1316019 | solution.py:134
  412.0 5.6 copy.142
  417.7 4.7 rev.6
  424.0 83.7 %reduce-scatter.5.cloned.1.call-done = bf16[8,1024]{1,0:T(8,128)(2,1)} async-done(((bf16[256,1024]{1,0:T(8,128)(2,1)}), bf16[8,1024]{1,0:T(8,128)(2,1)}) %reduce-scatter.5.cloned.1.call-update) | async-done | bytes 16400 | tf_op jit(solution)/shard_map/reduce_scatter | solution.py:213
  509.0 63.3 %all-gather.15.cloned.1.call-done = f32[64,128,128]{2,1,0:T(8,128)} async-done(((f32[2,128,128]{2,1,0:T(8,128)}), f32[64,128,128]{2,1,0:T(8,128)}) %all-gather.15.cloned.1.call-update) | async-done | bytes 4194320 | tf_op jit(solution)/shard_map/all_gather | solution.py:23
  572.4 5.6 copy.145
  578.0 4.7 rev.7
  582.6 40.0 %while.148 = (s32[]{:T(128)}, f32[2,128,128]{1,2,0:T(8,128)S(1)}, s32[]{:T(128)}, f32[32,2,128,128]{2,3,1,0:T(8,128)}, f32[32,2,128,128]{2,3,1,0:T(8,128)}, /*index=5*/s32[]{:T(128)}, s32[]{:T(128)}) while((s32[]{:T(128)}, f32[2,128,128]{1,2,0:T(8,128)S(1)}, s32[]{:T(128)}, f32[32,2,128,128]{2,3,1,0:T(8,128)}, ...), condition=%wide.region_16.18_spmd.clone, body=%wide.region_15.17_spmd.clone.sunk | while | flops 50462724 | bytes 920167 | solution.py:35
  624.9 133.3 %while.144 = (s32[]{:T(128)}, f32[2,128,128]{2,1,0:T(8,128)S(1)}, f32[4,2,64,128]{3,2,1,0:T(8,128)}, f32[4,2,64,128]{3,2,1,0:T(8,128)}, f32[4,2,64,128]{3,2,1,0:...) while((s32[]{:T(128)}, f32[2,128,128]{2,1,0:T(8,128)S(1)}, ...), condition=%wide.region_28.30_spmd.clone.clone, body=%wide.region_17.29_spmd.clone.clone.sunk | while | flops 283874368 | bytes 5498349 | solution.py:134
  627.6 1.5 add_bitcast_fusion.3
  629.1 10.6 %custom-call.43 = f32[2,1,64,64]{2,3,1,0:T(8,128)S(1)} custom-call(f32[2,1,64,64]{3,2,1,0:T(8,128)} %add_bitcast_fusion.3), custom_call_target="InvertDiagBlocksLowerTriangular" | custom-call | tf_op jit(solution)/shard_map/transpose(jvp())/while/body/eval_jaxpr/triangular_solve | solution.py:103
  645.5 1.7 fusion.359
  653.3 1.7 fusion.369
  660.9 1.5 add_bitcast_fusion.3
  662.4 10.6 %custom-call.43 = f32[2,1,64,64]{2,3,1,0:T(8,128)S(1)} custom-call(f32[2,1,64,64]{3,2,1,0:T(8,128)} %add_bitcast_fusion.3), custom_call_target="InvertDiagBlocksLowerTriangular" | custom-call | tf_op jit(solution)/shard_map/transpose(jvp())/while/body/eval_jaxpr/triangular_solve | solution.py:103
  678.9 1.7 fusion.359
  686.6 1.7 fusion.369
  695.7 10.6 %custom-call.43 = f32[2,1,64,64]{2,3,1,0:T(8,128)S(1)} custom-call(f32[2,1,64,64]{3,2,1,0:T(8,128)} %add_bitcast_fusion.3), custom_call_target="InvertDiagBlocksLowerTriangular" | custom-call | tf_op jit(solution)/shard_map/transpose(jvp())/while/body/eval_jaxpr/triangular_solve | solution.py:103
  712.1 1.7 fusion.359
  719.9 1.7 fusion.369
  729.0 10.6 %custom-call.43 = f32[2,1,64,64]{2,3,1,0:T(8,128)S(1)} custom-call(f32[2,1,64,64]{3,2,1,0:T(8,128)} %add_bitcast_fusion.3), custom_call_target="InvertDiagBlocksLowerTriangular" | custom-call | tf_op jit(solution)/shard_map/transpose(jvp())/while/body/eval_jaxpr/triangular_solve | solution.py:103
  745.5 1.7 fusion.359
  753.2 1.7 fusion.369
  763.2 1.5 multiply_reduce_fusion.3
  765.4 4.1 collective-permute-start.1
  770.9 55.8 %all-reduce.15 = (f32[4,512]{1,0:T(4,128)}, f32[128]{0:T(128)S(1)}) all-reduce(f32[4,512]{1,0:T(4,128)S(1)} %pad_add_fusion.5, f32[128]{0:T(128)S(1)} %copy-done.26), channel_id=1, replica_groups=mesh['dp'=8,'ctx'=32] {'ctx'}, use_global_device_ids=true, to_apply=%region_37.39 | all-reduce | flops 2176 | bytes 17408 | tf_op jit(solution)/shard_map/psum | solution.py:233
  826.7 23.8 %psum.23 = f32[128]{0:T(128)} all-reduce(f32[128]{0:T(128)S(1)} %get-tuple-element.2610), channel_id=1, replica_groups=mesh['dp'=8,'ctx'=32] {'dp'}, use_global_device_ids=true, to_apply=%region_41.43 | all-reduce | flops 128 | bytes 1024 | tf_op jit(solution)/shard_map/psum | solution.py:234
  (653 shorter events, 296.4 us)
Async XLA Ops:
  7.2 103.3 %copy-start = (bf16[256,1024]{1,0:T(8,128)(2,1)S(1)}, bf16[256,1024]{1,0:T(8,128)(2,1)}, u32[]{:S(2)}) copy-start(bf16[256,1024]{1,0:T(8,128)(2,1)} %param.28) | copy-start | bytes 1572868
  7.2 133.1 %all-gather.9.cloned.1.call-start = ((), (), s32[]{:S(2)}) async-start(), calls=%async_computation.4 | async-start | bytes 4325376 | tf_op jit(solution)/shard_map/all_gather | solution.py:23
  8.0 8.4 collective-permute-start
  11.5 7.5 copy-start.14
  11.5 7.5 copy-start.16
  11.5 7.5 copy-start.18
  11.5 8.7 %copy-start.12 = (f32[1,512]{1,0:T(1,128)}, f32[1,512]{1,0:T(1,128)S(1)}, u32[]{:S(2)}) copy-start(f32[1,512]{1,0:T(1,128)S(1)} %get-tuple-element.2670) | copy-start | bytes 6148
  18.7 0.6 copy-start.21
  18.7 0.6 copy-start.22
  18.8 1.3 copy-start.20
  20.1 54.2 %copy-start.9 = (bf16[32,1024]{1,0:T(8,128)(2,1)S(1)}, bf16[32,1024]{1,0:T(8,128)(2,1)}, u32[]{:S(2)}) copy-start(bf16[32,1024]{1,0:T(8,128)(2,1)} %param.29) | copy-start | bytes 196612
  20.2 91.5 %copy-start.24 = (f32[128]{0:T(128)S(1)}, f32[128]{0:T(128)}, u32[]{:S(2)}) copy-start(f32[128]{0:T(128)} %param.27) | copy-start | bytes 1540
  72.5 39.2 %copy-start.2 = (f32[2,128,128]{1,2,0:T(8,128)}, f32[2,128,128]{1,2,0:T(8,128)S(1)}, u32[]{:S(2)}) copy-start(f32[2,128,128]{1,2,0:T(8,128)S(1)} %get-tuple-element.1689) | copy-start | bytes 393220
  72.5 136.3 %copy-start.8 = (f32[4,2,64]{2,1,0:T(2,128)}, f32[4,2,64]{2,1,0:T(2,128)S(1)}, u32[]{:S(2)}) copy-start(f32[4,2,64]{2,1,0:T(2,128)S(1)} %get-tuple-element.3692) | copy-start | bytes 6148
  72.5 136.3 %copy-start.10 = (f32[4,2,64]{2,1,0:T(2,128)}, f32[4,2,64]{2,1,0:T(2,128)S(1)}, u32[]{:S(2)}) copy-start(f32[4,2,64]{2,1,0:T(2,128)S(1)} %get-tuple-element.3696) | copy-start | bytes 6148
  73.3 135.5 %all-gather.11.cloned.1.call-start = ((), (), s32[]{:S(2)}) async-start(), calls=%async_computation.5 | async-start | bytes 4325376 | tf_op jit(solution)/shard_map/all_gather | solution.py:23
  74.1 337.9 %all-gather.13.cloned.1.call-start = ((), (), s32[]{:S(2)}) async-start(), calls=%async_computation.6 | async-start | bytes 4325376 | tf_op jit(solution)/shard_map/all_gather | solution.py:23
  109.6 0.8 copy-start.3
  110.8 0.8 copy-start.4
  111.7 396.0 %reduce-scatter.5.cloned.1.call-start = ((), (), s32[]{:S(2)}) async-start(), calls=%async_computation.3 | async-start | bytes 540672 | tf_op jit(solution)/shard_map/reduce_scatter | solution.py:213
  208.8 78.2 %copy-start.11 = (f32[4,2,64,1]{2,1,3,0:T(2,128)S(1)}, f32[4,2,64,1]{2,1,3,0:T(2,128)}, u32[]{:S(2)}) copy-start(f32[4,2,64,1]{2,1,3,0:T(2,128)} %custom-call.36) | copy-start | bytes 6148
  287.1 97.9 %copy-start.25 = (f32[128]{0:T(128)S(1)}, f32[128]{0:T(128)}, u32[]{:S(2)}) copy-start(f32[128]{0:T(128)} %param.27) | copy-start | bytes 1540
  390.1 2.3 copy-start.5
  392.3 180.1 %all-gather.15.cloned.1.call-start = ((), (), s32[]{:S(2)}) async-start(), calls=%async_computation.7 | async-start | bytes 4325376 | tf_op jit(solution)/shard_map/all_gather | solution.py:23
  411.0 0.7 copy-start.1
  411.7 439.1 %reduce-scatter.3.cloned.1.call-start = ((), (), s32[]{:S(2)}) async-start(), calls=%async_computation.2 | async-start | bytes 589824 | tf_op jit(solution)/shard_map/reduce_scatter | solution.py:205
  417.7 5.2 copy-start.6
  758.2 6.6 copy-start.13
  758.2 6.6 copy-start.15
  758.2 6.6 copy-start.17
  758.2 6.6 copy-start.19
  764.7 5.6 copy-start.23
  764.7 6.2 copy-start.26
  765.4 85.1 %collective-permute-start.1 = (f32[3,512]{1,0:T(4,128)S(1)}, f32[3,512]{1,0:T(4,128)S(1)}, u32[]{:S(2)}, u32[]{:S(2)}) collective-permute-start(f32[3,512]{1,0:T(4,128)S(1)} %pad_add_fusion.4), channel_id=1, source_target_pairs={{1,0},{2,1},{3,2},{4,3},{5,4},{6,5},{7,6},{8,7},{9,8},{10,9},{11,1... | collective-permute-start | bytes 18440 | tf_op jit(solution)/shard_map/ppermute | solution.py:18
  850.7 0.7 copy-start.7
Sparse Core Ops, SparseCore 0:
  73.4 66.8 all-gather.8
  142.2 66.6 all-gather.10
  210.7 66.4 all-gather.12
  392.4 115.2 reduce-scatter.4
  509.6 62.7 all-gather.14
  577.2 75.5 reduce-scatter.2
where the time goes:
time: 865 us; the launch traced here: 858 us
  waiting for transfers between devices  248 us (29%)
  matrix products  195 us (23%)
  other arithmetic  179 us (21%)
  blocking collectives  115 us (13%)
  local copies, waits for them, and re-layouts  95.8 us (11%)
  between operations  14.9 us (2%)
    dot_general x170, matrix products, product(): return jnp.einsum(pattern, left_array, right_array, precision=HIGHEST)  172 us
    all_gather x4, waiting for transfers between devices, prefix_2(): pieces = jax.tree.map(lambda part: lax.all_gather(part, axis), value)  160 us
    another operation x48, other arithmetic, block_terms(): lax.linalg.triangular_solve(lower_mat, stacked, left_side=True, lower=Tru...  133 us
    reduce_scatter x1, waiting for transfers between devices, local(): lax.psum_scatter(jnp.einsum('tv,td->vd', normed, full_grad, preferred_ele...  83.7 us
    psum x1, blocking collectives, local(): grad_conv_total, gain_partial = lax.psum((grad_conv, grad_gain), 'ctx')  55.8 us
    all_gather x1, blocking collectives, local(): full_grad = lax.all_gather(out_grad, 'dp', axis=0, tiled=True)  35.2 us
    dynamic_slice x62, local copies, waits for them, and re-layouts, step(): longer = join(total, jax.tree.map(lambda part: part[position], pieces))  31.4 us
    psum x1, blocking collectives, local(): grad_gain_total = lax.psum(gain_partial, 'dp')  23.8 us
  transfers between devices with their start and end apart: 8, of which 5 were waited for; matrix products, arithmetic and copies ran while one was open for 48% of the time, Pallas kernels for 0%

commit v1 on v0

--- a/solution.py
+++ b/solution.py
@@ -208,7 +208,9 @@
         scatter_dimension=0,
         tiled=True,
     )
-    full_grad = lax.all_gather(out_grad, "dp", axis=0, tiled=True)
+    full_grad = jnp.concatenate(
+        lax.all_to_all(jnp.stack([out_grad] * lax.axis_size("dp")), "dp", 0, 0), axis=0
+    )
     back_rows = jnp.dot(full_grad, out_weight.T, preferred_element_type=jnp.float32)
     grad_weight = lax.psum_scatter(
         jnp.einsum("tv,td->vd", normed, full_grad, preferred_element_type=jnp.float32).astype(

time: 865 us -> 833 us (0.963)
  blocking collectives: 115 us -> 79.6 us
  waiting for transfers between devices: 248 us -> 276 us
  other arithmetic: 179 us -> 156 us
    all_gather x1 -> x0, blocking collectives: 35.2 us -> none  [local(): full_grad = lax.all_gather(out_grad, 'dp', axis=0, tiled=True)]
    all_gather x4, waiting for transfers between devices: 160 us -> 190 us  [prefix_2(): pieces = jax.tree.map(lambda part: lax.all_gather(part, axis), value)]
    another operation x48, other arithmetic: 133 us -> 122 us  [block_terms(): lax.linalg.triangular_solve(lower_mat, stacked, left_side=True, lower=Tru...]
  transfers between devices with their start and end apart: 8 -> 9, of which waited for: 5 -> 5; matrix products, arithmetic and copies ran while one was open for 48% -> 46% of each run, Pallas kernels for 0% -> 0%
where the time goes in v1:
time: 833 us; the launch traced here: 827 us
  waiting for transfers between devices  276 us (33%)
  matrix products  192 us (23%)
  other arithmetic  156 us (19%)
  local copies, waits for them, and re-layouts  91.5 us (11%)
  blocking collectives  79.6 us (10%)
  between operations  14.9 us (2%)
  starting transfers between devices  12.8 us (2%)
    all_gather x4, waiting for transfers between devices, prefix_2(): pieces = jax.tree.map(lambda part: lax.all_gather(part, axis), value)  190 us
    dot_general x170, matrix products, product(): return jnp.einsum(pattern, left_array, right_array, precision=HIGHEST)  169 us
    another operation x48, other arithmetic, block_terms(): lax.linalg.triangular_solve(lower_mat, stacked, left_side=True, lower=Tru...  122 us
    reduce_scatter x1, waiting for transfers between devices, local(): lax.psum_scatter(jnp.einsum('tv,td->vd', normed, full_grad, preferred_ele...  82 us
    psum x1, blocking collectives, local(): grad_conv_total, gain_partial = lax.psum((grad_conv, grad_gain), 'ctx')  55.8 us
    dynamic_slice x62, local copies, waits for them, and re-layouts, step(): longer = join(total, jax.tree.map(lambda part: part[position], pieces))  31.4 us
    psum x1, blocking collectives, local(): grad_gain_total = lax.psum(gain_partial, 'dp')  23.8 us
  transfers between devices with their start and end apart: 9, of which 5 were waited for; matrix products, arithmetic and copies ran while one was open for 46% of the time, Pallas kernels for 0%

profile of v1, /device:TPU:8, one launch (start us, length us, event | category | flops | bytes accessed | tf_op | source)
XLA Modules:
  0.0 827.1 jit_solution(1264442451991390190)
XLA Ops:
  8.0 1.9 collective-permute-start
  12.5 3.9 collective-permute-done
  19.4 52.3 %while.145 = (s32[]{:T(128)}, f32[2,128,128]{1,2,0:T(8,128)S(1)}, f32[2,128,128]{1,2,0:T(8,128)S(1)}, f32[4,2,64]{2,1,0:T(2,128)S(1)}, f32[4,2,64]{2,1,0:T(2,128...) while((s32[]{:T(128)}, f32[2,128,128]{1,2,0:T(8,128)S(1)}, ...), condition=%wide.region_3.5_spmd.clone, body=%wide.region_1.4_spmd.clone.sunk | while | flops 189067456 | bytes 2523323 | solution.py:168
  20.3 9.8 %custom-call.44 = f32[2,1,64,64]{2,3,1,0:T(8,128)S(1)} custom-call(f32[2,1,64,64]{3,2,1,0:T(8,128)S(1)} %fusion.389), custom_call_target="InvertDiagBlocksLowerTriangular" | custom-call | tf_op jit(solution)/shard_map/while/body/eval_jaxpr/triangular_solve/custom-call.1 | solution.py:103
  33.4 9.8 %custom-call.44 = f32[2,1,64,64]{2,3,1,0:T(8,128)S(1)} custom-call(f32[2,1,64,64]{3,2,1,0:T(8,128)S(1)} %fusion.389), custom_call_target="InvertDiagBlocksLowerTriangular" | custom-call | tf_op jit(solution)/shard_map/while/body/eval_jaxpr/triangular_solve/custom-call.1 | solution.py:103
  46.5 9.8 %custom-call.44 = f32[2,1,64,64]{2,3,1,0:T(8,128)S(1)} custom-call(f32[2,1,64,64]{3,2,1,0:T(8,128)S(1)} %fusion.389), custom_call_target="InvertDiagBlocksLowerTriangular" | custom-call | tf_op jit(solution)/shard_map/while/body/eval_jaxpr/triangular_solve/custom-call.1 | solution.py:103
  59.6 9.8 %custom-call.44 = f32[2,1,64,64]{2,3,1,0:T(8,128)S(1)} custom-call(f32[2,1,64,64]{3,2,1,0:T(8,128)S(1)} %fusion.389), custom_call_target="InvertDiagBlocksLowerTriangular" | custom-call | tf_op jit(solution)/shard_map/while/body/eval_jaxpr/triangular_solve/custom-call.1 | solution.py:103
  74.2 6.3 all-to-all-start
  81.3 58.9 %all-gather.9.cloned.1.call-done = f32[64,128,128]{2,1,0:T(8,128)} async-done(((f32[2,128,128]{2,1,0:T(8,128)}), f32[64,128,128]{2,1,0:T(8,128)}) %all-gather.9.cloned.1.call-update) | async-done | bytes 4194320 | tf_op jit(solution)/shard_map/all_gather | solution.py:23
  140.2 67.6 %all-gather.11.cloned.1.call-done = f32[64,128,128]{2,1,0:T(8,128)} async-done(((f32[2,128,128]{2,1,0:T(8,128)}), f32[64,128,128]{2,1,0:T(8,128)}) %all-gather.11.cloned.1.call-update) | async-done | bytes 4194320 | tf_op jit(solution)/shard_map/all_gather | solution.py:23
  207.8 73.6 %while.146 = (s32[]{:T(128)}, f32[2,128,128]{1,2,0:T(8,128)S(1)}, s32[]{:T(128)}, f32[32,2,128,128]{3,2,1,0:T(8,128)}, f32[32,2,128,128]{3,2,1,0:T(8,128)}, /*index=5*/s32[]{:T(128)}, s32[]{:T(128)}) while((s32[]{:T(128)}, f32[2,128,128]{1,2,0:T(8,128)S(1)}, s32[]{:T(128)}, f32[32,2,128,128]{3,2,1,0:T(8,128)}, ...), condition=%wide.region_5.7_spmd.clone, body=%wide.region_4.6_spmd.clone.sunk | while | flops 50462724 | bytes 1443939 | solution.py:35
  225.5 1.3 fusion.393
  239.7 1.3 fusion.393
  265.8 1.3 fusion.393
  284.5 76.2 %while.143 = (s32[]{:T(128)}, f32[2,128,128]{2,1,0:T(8,128)S(1)}, f32[4,2,64,128]{3,2,1,0:T(8,128)S(1)}, f32[4,2,64,64]{3,2,1,0:T(8,128)}, f32[4,2,64,64]{3,2,1,...) while((s32[]{:T(128)}, f32[2,128,128]{2,1,0:T(8,128)S(1)}, ...), condition=%wide.region_9.11_spmd.clone.clone, body=%wide.region_7.10_spmd.clone.clone.sunk | while | flops 138834496 | bytes 3690345 | solution.py:134
  287.0 9.8 %custom-call.42 = f32[2,1,64,64]{2,3,1,0:T(8,128)S(1)} custom-call(f32[2,1,64,64]{3,2,1,0:T(8,128)S(1)} %get-tuple-element.3142), custom_call_target="InvertDiagBlocksLowerTriangular" | custom-call | tf_op jit(solution)/shard_map/jvp()/while/body/eval_jaxpr/triangular_solve/custom-call.1 | solution.py:103
  306.0 9.8 %custom-call.42 = f32[2,1,64,64]{2,3,1,0:T(8,128)S(1)} custom-call(f32[2,1,64,64]{3,2,1,0:T(8,128)S(1)} %get-tuple-element.3142), custom_call_target="InvertDiagBlocksLowerTriangular" | custom-call | tf_op jit(solution)/shard_map/jvp()/while/body/eval_jaxpr/triangular_solve/custom-call.1 | solution.py:103
  325.0 9.8 %custom-call.42 = f32[2,1,64,64]{2,3,1,0:T(8,128)S(1)} custom-call(f32[2,1,64,64]{3,2,1,0:T(8,128)S(1)} %get-tuple-element.3142), custom_call_target="InvertDiagBlocksLowerTriangular" | custom-call | tf_op jit(solution)/shard_map/jvp()/while/body/eval_jaxpr/triangular_solve/custom-call.1 | solution.py:103
  344.1 9.8 %custom-call.42 = f32[2,1,64,64]{2,3,1,0:T(8,128)S(1)} custom-call(f32[2,1,64,64]{3,2,1,0:T(8,128)S(1)} %get-tuple-element.3142), custom_call_target="InvertDiagBlocksLowerTriangular" | custom-call | tf_op jit(solution)/shard_map/jvp()/while/body/eval_jaxpr/triangular_solve/custom-call.1 | solution.py:103
  361.0 2.0 fusion.222
  363.6 2.2 convolution_convert_fusion
  365.8 18.7 %while.147 = (s32[]{:T(128)}, f32[2,128,128]{2,1,0:T(8,128)S(1)}, f32[4,2,1,1]{1,3,2,0:T(1,128)}, f32[4,2,64,1]{2,1,3,0:T(2,128)S(1)}, f32[4,2,64,128]{3,2,1,0:T...) while((s32[]{:T(128)}, f32[2,128,128]{2,1,0:T(8,128)S(1)}, ...), condition=%wide.region_14.16_spmd.clone, body=%wide.region_13.15_spmd.clone.sunk | while | flops 88293376 | bytes 1316011 | solution.py:134
  385.7 5.6 copy.108
  391.4 4.6 rev.6
  396.8 2.0 convolution_convert_fusion.1
  398.9 82.0 %reduce-scatter.5.cloned.1.call-done = bf16[8,1024]{1,0:T(8,128)(2,1)} async-done(((bf16[256,1024]{1,0:T(8,128)(2,1)}), bf16[8,1024]{1,0:T(8,128)(2,1)}) %reduce-scatter.5.cloned.1.call-update) | async-done | bytes 16400 | tf_op jit(solution)/shard_map/reduce_scatter | solution.py:215
  480.9 1.3 convert_element_type.41
  482.2 63.4 %all-gather.15.cloned.1.call-done = f32[64,128,128]{2,1,0:T(8,128)} async-done(((f32[2,128,128]{2,1,0:T(8,128)}), f32[64,128,128]{2,1,0:T(8,128)}) %all-gather.15.cloned.1.call-update) | async-done | bytes 4194320 | tf_op jit(solution)/shard_map/all_gather | solution.py:23
  545.6 5.6 copy.112
  551.2 4.7 rev.7
  555.8 40.0 %while.148 = (s32[]{:T(128)}, f32[2,128,128]{1,2,0:T(8,128)S(1)}, s32[]{:T(128)}, f32[32,2,128,128]{2,3,1,0:T(8,128)}, f32[32,2,128,128]{2,3,1,0:T(8,128)}, /*index=5*/s32[]{:T(128)}, s32[]{:T(128)}) while((s32[]{:T(128)}, f32[2,128,128]{1,2,0:T(8,128)S(1)}, s32[]{:T(128)}, f32[32,2,128,128]{2,3,1,0:T(8,128)}, ...), condition=%wide.region_16.18_spmd.clone, body=%wide.region_15.17_spmd.clone.sunk | while | flops 50462724 | bytes 920159 | solution.py:35
  599.3 127.7 %while.144 = (s32[]{:T(128)}, f32[2,128,128]{2,1,0:T(8,128)S(1)}, f32[4,2,64,128]{3,2,1,0:T(8,128)}, f32[4,2,64,128]{3,2,1,0:T(8,128)}, f32[4,2,64,128]{3,2,1,0:...) while((s32[]{:T(128)}, f32[2,128,128]{2,1,0:T(8,128)S(1)}, ...), condition=%wide.region_28.30_spmd.clone.clone, body=%wide.region_17.29_spmd.clone.clone.sunk | while | flops 283874368 | bytes 5495781 | solution.py:134
  605.1 9.8 %custom-call.43 = f32[2,1,64,64]{2,3,1,0:T(8,128)S(1)} custom-call(f32[2,1,64,64]{3,2,1,0:T(8,128)S(1)} %add_bitcast_fusion.3), custom_call_target="InvertDiagBlocksLowerTriangular" | custom-call | tf_op jit(solution)/shard_map/transpose(jvp())/while/body/eval_jaxpr/triangular_solve | solution.py:103
  624.6 1.7 fusion.374
  629.6 1.7 fusion.364
  637.0 9.8 %custom-call.43 = f32[2,1,64,64]{2,3,1,0:T(8,128)S(1)} custom-call(f32[2,1,64,64]{3,2,1,0:T(8,128)S(1)} %add_bitcast_fusion.3), custom_call_target="InvertDiagBlocksLowerTriangular" | custom-call | tf_op jit(solution)/shard_map/transpose(jvp())/while/body/eval_jaxpr/triangular_solve | solution.py:103
  656.5 1.7 fusion.374
  661.6 1.7 fusion.364
  668.9 9.8 %custom-call.43 = f32[2,1,64,64]{2,3,1,0:T(8,128)S(1)} custom-call(f32[2,1,64,64]{3,2,1,0:T(8,128)S(1)} %add_bitcast_fusion.3), custom_call_target="InvertDiagBlocksLowerTriangular" | custom-call | tf_op jit(solution)/shard_map/transpose(jvp())/while/body/eval_jaxpr/triangular_solve | solution.py:103
  688.4 1.7 fusion.374
  693.4 1.7 fusion.364
  700.8 9.8 %custom-call.43 = f32[2,1,64,64]{2,3,1,0:T(8,128)S(1)} custom-call(f32[2,1,64,64]{3,2,1,0:T(8,128)S(1)} %add_bitcast_fusion.3), custom_call_target="InvertDiagBlocksLowerTriangular" | custom-call | tf_op jit(solution)/shard_map/transpose(jvp())/while/body/eval_jaxpr/triangular_solve | solution.py:103
  720.3 1.7 fusion.374
  725.3 1.7 fusion.364
  732.1 1.5 multiply_reduce_fusion.3
  733.9 4.1 collective-permute-start.1
  739.8 55.8 %all-reduce.15 = (f32[4,512]{1,0:T(4,128)}, f32[128]{0:T(128)S(1)}) all-reduce(f32[4,512]{1,0:T(4,128)S(1)} %pad_add_fusion.5, f32[128]{0:T(128)S(1)} %copy-done.20), channel_id=1, replica_groups=mesh['dp'=8,'ctx'=32] {'ctx'}, use_global_device_ids=true, to_apply=%region_37.39 | all-reduce | flops 2176 | bytes 17408 | tf_op jit(solution)/shard_map/psum | solution.py:235
  795.5 23.8 %psum.23 = f32[128]{0:T(128)} all-reduce(f32[128]{0:T(128)S(1)} %get-tuple-element.2523), channel_id=1, replica_groups=mesh['dp'=8,'ctx'=32] {'dp'}, use_global_device_ids=true, to_apply=%region_40.42 | all-reduce | flops 128 | bytes 1024 | tf_op jit(solution)/shard_map/psum | solution.py:236
  (648 shorter events, 275.8 us)
Async XLA Ops:
  7.2 353.8 %copy-start = (bf16[256,1024]{1,0:T(8,128)(2,1)S(1)}, bf16[256,1024]{1,0:T(8,128)(2,1)}, u32[]{:S(2)}) copy-start(bf16[256,1024]{1,0:T(8,128)(2,1)} %param.28) | copy-start | bytes 1572868
  7.2 133.0 %all-gather.9.cloned.1.call-start = ((), (), s32[]{:S(2)}) async-start(), calls=%async_computation.5 | async-start | bytes 4325376 | tf_op jit(solution)/shard_map/all_gather | solution.py:23
  8.0 8.4 %collective-permute-start = (bf16[3,512]{1,0:T(4,128)(2,1)S(1)}, bf16[3,512]{1,0:T(4,128)(2,1)S(1)}, u32[]{:S(2)}, u32[]{:S(2)}) collective-permute-start(bf16[3,512]{1,0:T(4,128)(2,1)S(1)} %slice.122), channel_id=1, source_target_pairs={{0,1},{1,2},{2,3},{3,4},{4,5},{5,6},{6,7},{7,8},{8,9},{9,10},{10,1... | collective-permute-start | bytes 9224 | tf_op jit(solution)/shard_map/ppermute | solution.py:18
  10.8 8.4 %copy-start.9 = (f32[1,512]{1,0:T(1,128)}, f32[1,512]{1,0:T(1,128)S(1)}, u32[]{:S(2)}) copy-start(f32[1,512]{1,0:T(1,128)S(1)} %get-tuple-element.2583) | copy-start | bytes 6148
  10.8 8.4 %copy-start.11 = (f32[1,512]{1,0:T(1,128)}, f32[1,512]{1,0:T(1,128)S(1)}, u32[]{:S(2)}) copy-start(f32[1,512]{1,0:T(1,128)S(1)} %get-tuple-element.2584) | copy-start | bytes 6148
  18.6 0.9 copy-start.3
  18.7 0.7 copy-start.16
  18.7 0.7 copy-start.17
  18.8 0.6 copy-start.15
  19.2 54.2 %copy-start.8 = (bf16[32,1024]{1,0:T(8,128)(2,1)S(1)}, bf16[32,1024]{1,0:T(8,128)(2,1)}, u32[]{:S(2)}) copy-start(bf16[32,1024]{1,0:T(8,128)(2,1)} %param.29) | copy-start | bytes 196612
  71.7 9.0 %copy-start.2 = (f32[2,128,128]{1,2,0:T(8,128)}, f32[2,128,128]{1,2,0:T(8,128)S(1)}, u32[]{:S(2)}) copy-start(f32[2,128,128]{1,2,0:T(8,128)S(1)} %get-tuple-element.1689) | copy-start | bytes 393220
  72.5 135.3 %all-gather.11.cloned.1.call-start = ((), (), s32[]{:S(2)}) async-start(), calls=%async_computation.6 | async-start | bytes 4325376 | tf_op jit(solution)/shard_map/all_gather | solution.py:23
  74.2 286.8 %all-to-all-start = ((bf16[8,32,1024]{2,1,0:T(8,128)(2,1)}), bf16[8,32,1024]{2,1,0:T(8,128)(2,1)}, u32[]{:S(2)}, u32[]{:S(2)}) async-start(bf16[8,32,1024]{2,1,0:T(8,128)(2,1)} %stack.2), calls=%async_computation.1 | async-start | bytes 1048576 | tf_op jit(solution)/shard_map/all_to_all | solution.py:212
  80.5 305.2 %all-gather.13.cloned.1.call-start = ((), (), s32[]{:S(2)}) async-start(), calls=%async_computation.7 | async-start | bytes 4325376 | tf_op jit(solution)/shard_map/all_gather | solution.py:23
  81.3 399.6 %reduce-scatter.5.cloned.1.call-start = ((), (), s32[]{:S(2)}) async-start(), calls=%async_computation.4 | async-start | bytes 540672 | tf_op jit(solution)/shard_map/reduce_scatter | solution.py:215
  284.5 76.5 %copy-start.19 = (f32[128]{0:T(128)S(1)}, f32[128]{0:T(128)}, u32[]{:S(2)}) copy-start(f32[128]{0:T(128)} %param.27) | copy-start | bytes 1540
  360.7 5.1 copy-start.5
  360.7 5.1 copy-start.6
  365.8 179.8 %all-gather.15.cloned.1.call-start = ((), (), s32[]{:S(2)}) async-start(), calls=%async_computation.8 | async-start | bytes 4325376 | tf_op jit(solution)/shard_map/all_gather | solution.py:23
  384.5 0.7 copy-start.1
  385.2 434.4 %reduce-scatter.3.cloned.1.call-start = ((), (), s32[]{:S(2)}) async-start(), calls=%async_computation.3 | async-start | bytes 589824 | tf_op jit(solution)/shard_map/reduce_scatter | solution.py:205
  599.3 131.0 %copy-start.4 = (f32[256,1,512]{2,0,1:T(8,128)S(1)}, f32[256,1,512]{2,0,1:T(8,128)}, u32[]{:S(2)}) copy-start(f32[256,1,512]{2,0,1:T(8,128)} %copy-done.3) | copy-start | bytes 1572868
  727.0 6.6 copy-start.10
  727.0 6.6 copy-start.12
  733.5 4.8 copy-start.14
  733.5 4.9 copy-start.13
  733.6 5.6 copy-start.18
  733.6 6.2 copy-start.20
  733.9 85.5 %collective-permute-start.1 = (f32[3,512]{1,0:T(4,128)S(1)}, f32[3,512]{1,0:T(4,128)S(1)}, u32[]{:S(2)}, u32[]{:S(2)}) collective-permute-start(f32[3,512]{1,0:T(4,128)S(1)} %pad_add_fusion.4), channel_id=1, source_target_pairs={{1,0},{2,1},{3,2},{4,3},{5,4},{6,5},{7,6},{8,7},{9,8},{10,9},{11,1... | collective-permute-start | bytes 18440 | tf_op jit(solution)/shard_map/ppermute | solution.py:18
  819.5 0.7 copy-start.7
Sparse Core Ops, SparseCore 0:
  72.6 67.4 all-gather.8
  142.0 65.7 all-gather.10
  209.7 66.4 all-gather.12
  365.9 114.9 reduce-scatter.4
  482.7 62.8 all-gather.14
  550.4 75.5 reduce-scatter.2
